TPU v7x, 128 devices: a whole 4x4x4 slice. The times are simulated.
128 devices in a mesh: sec: 4 (over z), dev: 32 (over x, y, core).
Axes of the slice: x: 4, y: 4, z: 4, core: 2. Of those that a mesh axis runs over, the one named last changes fastest.
Arguments:
- x_input: bfloat16 [262144, 2048], P(('sec', 'dev'))
- log_decay: float32 [262144, 32], P(('sec', 'dev')), as said below
- b_input: bfloat16 [262144, 64], P(('sec', 'dev')), may hold values from -6 to 6
- c_input: bfloat16 [262144, 64], P(('sec', 'dev')), may hold values from -0.75 to 0.75
- skip_gain: float32 [32], replicated, may hold values from 0.5 to 2
- score_weight: bfloat16 [2048], replicated, may hold values from -0.125 to 0.125
- trace_lengths: int32 [4], replicated, may hold values from 1 to 131072, 262144 in all
- step_lengths: int32 [2048], replicated, may hold values from 1 to 512, 262144 in all
- step_slot: int32 [2048], replicated, may hold values from 0 to 2047, each once
Outputs:
- y_output: bfloat16 [262144, 2048], P(('sec', 'dev'))
- step_scores: float32 [2048], P(('sec', 'dev'))
Inputs may be any that keep to these rules, and one draw needn't show every extreme that they name: `trace_lengths`: the lengths sum to 262144; one trace has exactly 131072 tokens. `step_lengths`: the lengths sum to 262144; some step has exactly 512 tokens. `step_slot`: each slot is named by exactly one step. `log_decay`: every entry is negative.
All inputs are finite; a program needn't handle non-finite values.
Results may differ from a plain program's by a relative error of at most 0.0053.
Values sent between devices are 32-bit elements; how exact they have to be, the bound alone decides.
No kernel may reach another device: no remote copies, remote signals or barrier semaphores. Data moves between devices by JAX's collectives and lax.ppermute only.
A program may use at most 384 MiB of HBM per device.

v0:
```python
import jax
import jax.numpy as jnp
from jax import lax
from jax.sharding import Mesh
from jax.sharding import PartitionSpec as P

GROUP = 256
SEC_DEV = ("sec", "dev_0", "dev_1", "dev_2")


def filled_with(value, identity):
    return jax.tree.map(
        lambda a, e: jnp.broadcast_to(jnp.asarray(e, a.dtype), a.shape), value, identity
    )


def prefix_by_axis(value, axes, combine, identity):
    before = start = filled_with(value, identity)
    running = value
    for axis in reversed(axes):
        length, index = (lax.axis_size(axis), lax.axis_index(axis))
        pieces = jax.tree.map(lambda part: lax.all_gather(part, axis), running)
        inside, running = (start, start)
        for k in range(length):
            passed = k < index
            running = combine(running, jax.tree.map(lambda part: part[k], pieces))
            inside = jax.tree.map(lambda new, old: jnp.where(passed, new, old), running, inside)
        before = combine(inside, before)
    return before


def trace_ids(starts, positions):
    return jnp.sum((starts[None, :] <= positions[:, None]).astype(jnp.int32), axis=1)


def combine(early, late):
    return (early[0] * late[0], late[0][:, None, None] * early[1] + late[1])


def shards(
    x_input,
    log_decay,
    b_input,
    c_input,
    skip_gain,
    score_weight,
    trace_lengths,
    step_lengths,
    step_slot,
):
    rows = x_input.shape[0]
    heads = log_decay.shape[1]
    width = x_input.shape[1]
    head_size = width // heads
    state_size = b_input.shape[1]
    count = rows // GROUP
    index = lax.axis_index(SEC_DEV)
    base = index * rows
    starts = jnp.cumsum(trace_lengths) - trace_lengths
    positions = base + jnp.arange(rows, dtype=jnp.int32)
    trace = trace_ids(starts, positions).reshape(count, GROUP)
    prev = trace_ids(starts, base + jnp.arange(count, dtype=jnp.int32) * GROUP - 1)
    x_blocks = x_input.reshape(count, GROUP, heads, head_size)
    c_blocks = c_input.reshape(count, GROUP, state_size)
    inputs = (
        x_blocks,
        log_decay.reshape(count, GROUP, heads),
        b_input.reshape(count, GROUP, state_size),
        c_blocks,
        trace,
        prev,
    )
    order = jnp.arange(GROUP, dtype=jnp.int32)
    causal = order[:, None] >= order[None, :]
    lower_ones = causal.astype(jnp.float32)

    def local_block(held, item):
        state_local, factor_prod = held
        x_heads, decay_group, b_group, c_group, trace_group, prev_trace = item
        cum = jnp.dot(
            lower_ones,
            decay_group,
            precision=lax.Precision.HIGHEST,
            preferred_element_type=jnp.float32,
        )
        cum_heads = cum.T
        keep = causal & (trace_group[:, None] == trace_group[None, :])
        gram = jnp.dot(c_group, b_group.T, preferred_element_type=jnp.float32)
        diff = cum_heads[:, :, None] - cum_heads[:, None, :]
        weight = (gram[None] * jnp.exp(jnp.where(keep[None], diff, -jnp.inf))).astype(jnp.bfloat16)
        intra = jnp.einsum("hts,shp->thp", weight, x_heads, preferred_element_type=jnp.float32)
        to_end = (
            jnp.exp(cum[-1][None, :] - cum)
            * (trace_group == trace_group[-1]).astype(jnp.float32)[:, None]
        )
        scaled = (x_heads.astype(jnp.float32) * to_end[:, :, None]).astype(jnp.bfloat16)
        new_state = jnp.einsum("shp,sn->hpn", scaled, b_group, preferred_element_type=jnp.float32)
        carry = jnp.exp(cum) * (trace_group == prev_trace).astype(jnp.float32)[:, None]
        factor = carry[-1]
        following = (factor[:, None, None] * state_local + new_state, factor_prod * factor)
        return (following, (intra, state_local, factor_prod, carry))

    start_held = (
        jnp.zeros((heads, head_size, state_size), jnp.float32),
        jnp.ones((heads,), jnp.float32),
    )
    (state_end, factor_end), (intra, state_enter, factor_enter, carry) = lax.scan(
        local_block, start_held, inputs
    )
    own = (factor_end, state_end)
    identity = (
        jnp.ones((heads,), jnp.float32),
        jnp.zeros((heads, head_size, state_size), jnp.float32),
    )
    incoming = prefix_by_axis(own, SEC_DEV, combine, identity)
    state_in = incoming[1]
    full_state = (factor_enter[:, :, None, None] * state_in[None] + state_enter).astype(
        jnp.bfloat16
    )
    inter = (
        jnp.einsum("ktn,khpn->kthp", c_blocks, full_state, preferred_element_type=jnp.float32)
        * carry[..., None]
    )
    mixed = intra + inter + skip_gain[None, None, :, None] * x_blocks.astype(jnp.float32)
    y_output = mixed.astype(jnp.bfloat16).reshape(rows, width)
    score = jnp.dot(y_output, score_weight, preferred_element_type=jnp.float32)
    total_steps = step_slot.shape[0]
    step_starts = jnp.cumsum(step_lengths) - step_lengths
    step_ends = step_starts + step_lengths
    inside = (step_starts[None, :] <= positions[:, None]) & (
        positions[:, None] < step_ends[None, :]
    )
    token_slot = jnp.sum(jnp.where(inside, step_slot[None, :], 0), axis=1)
    column_block = min(512, total_steps)
    pieces = []
    for first_column in range(0, total_steps, column_block):
        span = min(column_block, total_steps - first_column)
        column_ids = first_column + jnp.arange(span, dtype=jnp.int32)
        table = (token_slot[:, None] == column_ids[None, :]).astype(jnp.float32)
        pieces.append(
            jnp.dot(
                score[None, :],
                table,
                precision=lax.Precision.HIGHEST,
                preferred_element_type=jnp.float32,
            )[0]
        )
    spread = jnp.concatenate(pieces, axis=0)
    devices = lax.axis_size(SEC_DEV)
    owned = total_steps // devices
    received = lax.all_to_all(
        spread.reshape(devices, owned), SEC_DEV, split_axis=0, concat_axis=0, tiled=True
    )
    sums = jnp.sum(received, axis=0)
    own_slots = index * owned + jnp.arange(owned, dtype=jnp.int32)
    own_lengths = jnp.sum(
        jnp.where(step_slot[None, :] == own_slots[:, None], step_lengths[None, :], 0), axis=1
    )
    step_scores = sums / own_lengths.astype(jnp.float32)
    return (y_output, step_scores)


def solution(mesh):
    torus = Mesh(
        mesh.devices.reshape(mesh.shape["sec"], 4, 4, 2), ("sec", "dev_0", "dev_1", "dev_2")
    )
    in_specs = (
        P(SEC_DEV, None),
        P(SEC_DEV, None),
        P(SEC_DEV, None),
        P(SEC_DEV, None),
        P(),
        P(),
        P(),
        P(),
        P(),
    )
    out_specs = (P(SEC_DEV, None), P(SEC_DEV))
    return jax.shard_map(
        shards, mesh=torus, in_specs=in_specs, out_specs=out_specs, check_vma=False
    )
```

profile of v0, /device:TPU:1, one launch (start us, length us, event | category | flops | bytes accessed | tf_op | source)
XLA Modules:
  0.0 403.7 jit_solution(2343306125567923856)
XLA Ops:
  9.0 24.4 %reshape.379 = bf16[8,256,32,64]{3,2,1,0:T(8,128)(2,1)} reshape(bf16[2048,2048]{1,0:T(8,128)(2,1)} %param.11) | data formatting | bytes 16777216 | tf_op jit(solution)/shard_map/reshape | solution.py:63
  33.4 19.5 %copy.40 = bf16[8,256,32,64]{1,3,2,0:T(8,128)(2,1)} copy(bf16[8,256,32,64]{3,2,1,0:T(8,128)(2,1)} %reshape.379) | data formatting | bytes 16777216
  54.5 86.5 %while.21 = (s32[]{:T(128)}, f32[32,64,64]{2,1,0:T(8,128)S(1)}, f32[32]{0:T(128)S(1)}, f32[8,256,32,64]{1,3,2,0:T(8,128)}, f32[8,32,64,64]{3,2,1,0:T(8,128)}, /*...) while((s32[]{:T(128)}, f32[32,64,64]{2,1,0:T(8,128)S(1)}, ...), condition=%wide.region_4.5_spmd.clone, body=%wide.region_3.4_spmd.clone.sunk | while | flops 379937856 | bytes 8534613 | solution.py:107
  55.8 1.2 compare_convert_fusion.3
  57.7 4.3 %bitcast_dynamic-update-slice_fusion.7 = f32[8,256,32,64]{1,3,2,0:T(8,128)} fusion(f32[8,256,32,64]{1,3,2,0:T(8,128)} %get-tuple-element.347, s32[]{:T(128)} %get-tuple-element.344, f32[32,256]{1,0:T(8,128)S(1)} %get-tuple-element.323, f32[256,256]{1,0:T(8,128)S(1)} %fusion.87, pred[256,256]{1,0:T(8,128)(4,1)S(1)} %fusion.88, ...), kind=kOutput, calls=%fused_computation.9.clone.1 | convolution fusion | flops 276824064 | bytes 3539968 | tf_op jit(solution)/shard_map/while/body/eval_jaxpr/hts,shp->thp/dot_general | solution.py:91
  63.6 1.8 convolution_add_fusion.2
  66.7 1.2 compare_convert_fusion.3
  68.6 4.3 %bitcast_dynamic-update-slice_fusion.7 = f32[8,256,32,64]{1,3,2,0:T(8,128)} fusion(f32[8,256,32,64]{1,3,2,0:T(8,128)} %get-tuple-element.347, s32[]{:T(128)} %get-tuple-element.344, f32[32,256]{1,0:T(8,128)S(1)} %get-tuple-element.323, f32[256,256]{1,0:T(8,128)S(1)} %fusion.87, pred[256,256]{1,0:T(8,128)(4,1)S(1)} %fusion.88, ...), kind=kOutput, calls=%fused_computation.9.clone.1 | convolution fusion | flops 276824064 | bytes 3539968 | tf_op jit(solution)/shard_map/while/body/eval_jaxpr/hts,shp->thp/dot_general | solution.py:91
  74.4 1.8 convolution_add_fusion.2
  77.5 1.2 compare_convert_fusion.3
  79.4 4.3 %bitcast_dynamic-update-slice_fusion.7 = f32[8,256,32,64]{1,3,2,0:T(8,128)} fusion(f32[8,256,32,64]{1,3,2,0:T(8,128)} %get-tuple-element.347, s32[]{:T(128)} %get-tuple-element.344, f32[32,256]{1,0:T(8,128)S(1)} %get-tuple-element.323, f32[256,256]{1,0:T(8,128)S(1)} %fusion.87, pred[256,256]{1,0:T(8,128)(4,1)S(1)} %fusion.88, ...), kind=kOutput, calls=%fused_computation.9.clone.1 | convolution fusion | flops 276824064 | bytes 3539968 | tf_op jit(solution)/shard_map/while/body/eval_jaxpr/hts,shp->thp/dot_general | solution.py:91
  85.2 1.8 convolution_add_fusion.2
  88.3 1.2 compare_convert_fusion.3
  90.3 4.3 %bitcast_dynamic-update-slice_fusion.7 = f32[8,256,32,64]{1,3,2,0:T(8,128)} fusion(f32[8,256,32,64]{1,3,2,0:T(8,128)} %get-tuple-element.347, s32[]{:T(128)} %get-tuple-element.344, f32[32,256]{1,0:T(8,128)S(1)} %get-tuple-element.323, f32[256,256]{1,0:T(8,128)S(1)} %fusion.87, pred[256,256]{1,0:T(8,128)(4,1)S(1)} %fusion.88, ...), kind=kOutput, calls=%fused_computation.9.clone.1 | convolution fusion | flops 276824064 | bytes 3539968 | tf_op jit(solution)/shard_map/while/body/eval_jaxpr/hts,shp->thp/dot_general | solution.py:91
  96.0 1.8 convolution_add_fusion.2
  99.1 1.2 compare_convert_fusion.3
  101.1 4.3 %bitcast_dynamic-update-slice_fusion.7 = f32[8,256,32,64]{1,3,2,0:T(8,128)} fusion(f32[8,256,32,64]{1,3,2,0:T(8,128)} %get-tuple-element.347, s32[]{:T(128)} %get-tuple-element.344, f32[32,256]{1,0:T(8,128)S(1)} %get-tuple-element.323, f32[256,256]{1,0:T(8,128)S(1)} %fusion.87, pred[256,256]{1,0:T(8,128)(4,1)S(1)} %fusion.88, ...), kind=kOutput, calls=%fused_computation.9.clone.1 | convolution fusion | flops 276824064 | bytes 3539968 | tf_op jit(solution)/shard_map/while/body/eval_jaxpr/hts,shp->thp/dot_general | solution.py:91
  106.8 1.8 convolution_add_fusion.2
  109.9 1.2 compare_convert_fusion.3
  111.9 4.2 %bitcast_dynamic-update-slice_fusion.7 = f32[8,256,32,64]{1,3,2,0:T(8,128)} fusion(f32[8,256,32,64]{1,3,2,0:T(8,128)} %get-tuple-element.347, s32[]{:T(128)} %get-tuple-element.344, f32[32,256]{1,0:T(8,128)S(1)} %get-tuple-element.323, f32[256,256]{1,0:T(8,128)S(1)} %fusion.87, pred[256,256]{1,0:T(8,128)(4,1)S(1)} %fusion.88, ...), kind=kOutput, calls=%fused_computation.9.clone.1 | convolution fusion | flops 276824064 | bytes 3539968 | tf_op jit(solution)/shard_map/while/body/eval_jaxpr/hts,shp->thp/dot_general | solution.py:91
  117.6 1.8 convolution_add_fusion.2
  122.6 4.2 %bitcast_dynamic-update-slice_fusion.7 = f32[8,256,32,64]{1,3,2,0:T(8,128)} fusion(f32[8,256,32,64]{1,3,2,0:T(8,128)} %get-tuple-element.347, s32[]{:T(128)} %get-tuple-element.344, f32[32,256]{1,0:T(8,128)S(1)} %get-tuple-element.323, f32[256,256]{1,0:T(8,128)S(1)} %fusion.87, pred[256,256]{1,0:T(8,128)(4,1)S(1)} %fusion.88, ...), kind=kOutput, calls=%fused_computation.9.clone.1 | convolution fusion | flops 276824064 | bytes 3539968 | tf_op jit(solution)/shard_map/while/body/eval_jaxpr/hts,shp->thp/dot_general | solution.py:91
  128.4 1.8 convolution_add_fusion.2
  133.4 4.3 %bitcast_dynamic-update-slice_fusion.7 = f32[8,256,32,64]{1,3,2,0:T(8,128)} fusion(f32[8,256,32,64]{1,3,2,0:T(8,128)} %get-tuple-element.347, s32[]{:T(128)} %get-tuple-element.344, f32[32,256]{1,0:T(8,128)S(1)} %get-tuple-element.323, f32[256,256]{1,0:T(8,128)S(1)} %fusion.87, pred[256,256]{1,0:T(8,128)(4,1)S(1)} %fusion.88, ...), kind=kOutput, calls=%fused_computation.9.clone.1 | convolution fusion | flops 276824064 | bytes 3539968 | tf_op jit(solution)/shard_map/while/body/eval_jaxpr/hts,shp->thp/dot_general | solution.py:91
  139.2 1.8 convolution_add_fusion.2
  144.8 3.5 all-reduce
  148.4 10.7 %all-gather.16.cloned.1.call-done = f32[64,64,64]{2,1,0:T(8,128)} async-done(((f32[32,64,64]{2,1,0:T(8,128)}), f32[64,64,64]{2,1,0:T(8,128)}) %all-gather.16.cloned.1.call-update) | async-done | bytes 1048592 | tf_op jit(solution)/shard_map/all_gather | solution.py:22
  159.1 2.9 fusion.58
  162.1 8.6 %all-reduce.1 = f32[128]{0:T(128)S(1)} all-reduce(f32[128]{0:T(128)S(1)} %get-tuple-element.232), channel_id=4, replica_groups=mesh['sec'=4,'dev_0'=4,'dev_1'=4,'dev_2'=2] {'dev_1'}, use_global_device_ids=true, to_apply=%add.1 | all-reduce | flops 128 | bytes 1024
  170.7 40.4 %all-gather.10.cloned.1.call-done = f32[4,32,64,64]{3,2,1,0:T(8,128)} async-done(((f32[1,32,64,64]{3,2,1,0:T(8,128)}), f32[4,32,64,64]{3,2,1,0:T(8,128)}) %all-gather.10.cloned.1.call-update) | async-done | bytes 2097168 | tf_op jit(solution)/shard_map/all_gather | solution.py:22
  211.2 3.5 slice_add_fusion.8
  214.7 7.6 %all-gather.3 = f32[4,1,32]{2,1,0:T(1,128)S(1)} all-gather(f32[1,1,32]{2,1,0:T(1,128)S(1)} %get-tuple-element.227), channel_id=1, replica_groups=mesh['sec'=4,'dev_0'=4,'dev_1'=4,'dev_2'=2] {'dev_0'}, dimensions={0}, use_global_device_ids=true | all-gather | bytes 640 | tf_op jit(solution)/shard_map/all_gather | solution.py:22
  222.4 40.9 %all-gather.12.cloned.1.call-done = f32[4,32,64,64]{3,2,1,0:T(8,128)} async-done(((f32[1,32,64,64]{3,2,1,0:T(8,128)}), f32[4,32,64,64]{3,2,1,0:T(8,128)}) %all-gather.12.cloned.1.call-update) | async-done | bytes 2097168 | tf_op jit(solution)/shard_map/all_gather | solution.py:22
  263.3 3.5 slice_add_fusion.4
  267.3 7.9 %all-gather.4 = f32[4,1,32]{2,1,0:T(1,128)S(1)} all-gather(f32[1,1,32]{2,1,0:T(1,128)S(1)} %get-tuple-element.223), channel_id=1, replica_groups=mesh['sec'=4,'dev_0'=4,'dev_1'=4,'dev_2'=2] {'sec'}, dimensions={0}, use_global_device_ids=true | all-gather | bytes 640 | tf_op jit(solution)/shard_map/all_gather | solution.py:22
  275.5 3.5 select_reduce_fusion
  279.0 36.8 %all-gather.14.cloned.1.call-done = f32[4,32,64,64]{3,2,1,0:T(8,128)} async-done(((f32[1,32,64,64]{3,2,1,0:T(8,128)}), f32[4,32,64,64]{3,2,1,0:T(8,128)}) %all-gather.14.cloned.1.call-update) | async-done | bytes 2097168 | tf_op jit(solution)/shard_map/all_gather | solution.py:22
  315.8 6.4 %fusion.57 = f32[32,64,64]{2,1,0:T(8,128)S(1)} fusion(f32[4,32,64,64]{3,2,1,0:T(8,128)} %all-gather.14.cloned.1.call-done, f32[4,32,64,64]{3,2,1,0:T(8,128)} %all-gather.10.cloned.1.call-done, f32[4,32,64,64]{3,2,1,0:T(8,128)} %all-gather.12.cloned.1.call-done, f32[64,64,64]{2,1,0:T(8,128)S(1)} %copy-done.1, f32[32]{0:T(128)S(1)} %get-tuple-element.213, ...), kind=kLoop, calls=%fused_computation.75 | loop fusion | flops 5767168 | bytes 7866510 | tf_op jit(solution)/shard_map/mul | solution.py:117
  322.2 16.3 %fusion.37 = bf16[8,256,32,64]{1,3,2,0:T(8,128)(2,1)} fusion(f32[8,256,32,64]{1,3,2,0:T(8,128)} %get-tuple-element.84, bf16[8,256,32,64]{1,3,2,0:T(8,128)(2,1)} %get-tuple-element.382, bf16[8,256,64,1]{2,1,3,0:T(8,128)(2,1)} %bitcast.170, f32[32]{0:T(128)S(1)} %copy-done.8, f32[8,256,32]{1,2,0:T(8,128)S(1)} %get-tuple-element.89, ...), kind=kOutput, calls=%fused_computation.50 | convolution fusion | flops 565182464 | bytes 38798464 | tf_op jit(solution)/shard_map/ktn,khpn->kthp/dot_general | solution.py:121
  338.5 15.4 %copy.44 = bf16[8,256,32,64]{1,0,3,2:T(8,128)(2,1)} copy(bf16[8,256,32,64]{1,3,2,0:T(8,128)(2,1)} %fusion.37) | data formatting | bytes 16777216 | tf_op jit(solution)/shard_map/convert_element_type | solution.py:125
  353.9 10.5 %copy.53 = bf16[256,8,8,256]{3,1,2,0:T(8,128)(2,1)} copy(bf16[256,8,8,256]{3,2,1,0:T(8,128)(2,1)} %bitcast.167) | data formatting | bytes 16777216
  364.4 4.6 %convolution_bitcast_fusion = f32[2048,1]{0,1:T(1,128)S(1)} fusion(bf16[2048,2048]{0,1:T(8,128)(2,1)} %bitcast.165, bf16[2048,1]{0,1:T(2,128)(2,1)S(1)} %reshape.369), kind=kOutput, calls=%fused_computation.63 | convolution fusion | flops 8388608 | bytes 8400896 | tf_op jit(solution)/shard_map/dot_general | solution.py:126
  368.9 1.4 fusion.40
  370.4 1.3 fusion.45
  371.8 1.4 fusion.43
  373.2 1.4 fusion.41
  375.4 8.6 %all-to-all-start = ((f32[128,1,16]{2,1,0:T(1,128)}), f32[128,1,16]{2,1,0:T(1,128)S(1)}, u32[]{:S(2)}, u32[]{:S(2)}) async-start(f32[128,1,16]{2,1,0:T(1,128)} %bitcast.32), calls=%async_computation | async-start | bytes 131072 | tf_op jit(solution)/shard_map/all_to_all | solution.py:151
  384.2 12.2 %copy.46 = bf16[2048,2048]{1,0:T(8,128)(2,1)} copy(bf16[2048,2048]{0,1:T(8,128)(2,1)} %bitcast.166) | data formatting | bytes 16777216
  (174 shorter events, 38.8 us)
Async XLA Ops:
  7.2 152.0 %all-gather.16.cloned.1.call-start = ((), (), s32[]{:S(2)}) async-start(), calls=%async_computation.4 | async-start | bytes 3145728 | tf_op jit(solution)/shard_map/all_gather | solution.py:22
  33.4 19.5 %copy-start.3 = (bf16[2048,64]{0,1:T(8,128)(2,1)S(1)}, bf16[2048,64]{0,1:T(8,128)(2,1)}, u32[]{:S(2)}) copy-start(bf16[2048,64]{0,1:T(8,128)(2,1)} %param.14) | copy-start | bytes 786436
  33.4 19.7 %copy-start.4 = (f32[2048,32]{0,1:T(8,128)S(1)}, f32[2048,32]{0,1:T(8,128)}, u32[]{:S(2)}) copy-start(f32[2048,32]{0,1:T(8,128)} %param.12) | copy-start | bytes 786436
  54.5 87.6 %copy-start.10 = (u32[128]{0:T(128)S(1)}, u32[128]{0:T(128)}, u32[]{:S(2)}) copy-start(u32[128]{0:T(128)} %constant.83) | copy-start | bytes 1540
  54.5 88.2 %copy-start.9 = (u32[128]{0:T(128)S(1)}, u32[128]{0:T(128)}, u32[]{:S(2)}) copy-start(u32[128]{0:T(128)} %constant.88) | copy-start | bytes 1540
  141.1 1.0 copy-start
  141.1 18.0 %copy-start.2 = (bf16[8,256,64]{2,1,0:T(8,128)(2,1)}, bf16[8,256,64]{2,1,0:T(8,128)(2,1)S(1)}, u32[]{:S(2)}) copy-start(bf16[8,256,64]{2,1,0:T(8,128)(2,1)S(1)} %get-tuple-element.393) | copy-start | bytes 786436
  142.1 69.1 %all-gather.10.cloned.1.call-start = ((), (), s32[]{:S(2)}) async-start(), calls=%async_computation.1 | async-start | bytes 5242880 | tf_op jit(solution)/shard_map/all_gather | solution.py:22
  159.1 107.8 %copy-start.7 = (bf16[2048]{0:T(1024)(128)(2,1)S(1)}, bf16[2048]{0:T(1024)(128)(2,1)}, u32[]{:S(2)}) copy-start(bf16[2048]{0:T(1024)(128)(2,1)} %param.16) | copy-start | bytes 12292
  159.1 107.8 %copy-start.5 = (s32[2048]{0:T(1024)S(1)}, s32[2048]{0:T(1024)}, u32[]{:S(2)}) copy-start(s32[2048]{0:T(1024)} %param.18) | copy-start | bytes 24580
  159.1 116.4 %copy-start.6 = (s32[2048]{0:T(1024)S(1)}, s32[2048]{0:T(1024)}, u32[]{:S(2)}) copy-start(s32[2048]{0:T(1024)} %param.19) | copy-start | bytes 24580
  159.1 156.6 %copy-start.1 = (f32[64,64,64]{2,1,0:T(8,128)S(1)}, f32[64,64,64]{2,1,0:T(8,128)}, u32[]{:S(2)}) copy-start(f32[64,64,64]{2,1,0:T(8,128)} %all-gather.16.cloned.1.call-done) | copy-start | bytes 3145732
  162.0 101.3 %all-gather.12.cloned.1.call-start = ((), (), s32[]{:S(2)}) async-start(), calls=%async_computation.2 | async-start | bytes 5242880 | tf_op jit(solution)/shard_map/all_gather | solution.py:22
  214.7 101.1 %all-gather.14.cloned.1.call-start = ((), (), s32[]{:S(2)}) async-start(), calls=%async_computation.3 | async-start | bytes 5242880 | tf_op jit(solution)/shard_map/all_gather | solution.py:22
  266.8 55.4 %copy-start.8 = (f32[32]{0:T(128)S(1)}, f32[32]{0:T(128)}, u32[]{:S(2)}) copy-start(f32[32]{0:T(128)} %param.15) | copy-start | bytes 388
  375.4 21.1 %all-to-all-start = ((f32[128,1,16]{2,1,0:T(1,128)}), f32[128,1,16]{2,1,0:T(1,128)S(1)}, u32[]{:S(2)}, u32[]{:S(2)}) async-start(f32[128,1,16]{2,1,0:T(1,128)} %bitcast.32), calls=%async_computation | async-start | bytes 131072 | tf_op jit(solution)/shard_map/all_to_all | solution.py:151
Sparse Core Ops, SparseCore 0:
  142.2 16.8 all-gather.15
  162.2 48.9 all-gather.9
  214.8 48.4 all-gather.11
  267.0 48.7 all-gather.13
where the time goes:
time: 406 us; the launch traced here: 404 us
  waiting for transfers between devices  129 us (32%)
  local copies, waits for them, and re-layouts  99.7 us (25%)
  matrix products  79.1 us (19%)
  other arithmetic  43.7 us (11%)
  blocking collectives  27.6 us (7%)
  between operations  15.3 us (4%)
  starting transfers between devices  8.78 us (2%)
    all_gather x4, waiting for transfers between devices, prefix_by_axis(): pieces = jax.tree.map(lambda part: lax.all_gather(part, axis), running)  129 us
    unnamed x33, local copies, waits for them, and re-layouts  45.2 us
    dot_general x8, matrix products, local_block(): jnp.einsum('hts,shp->thp', weight, x_heads, preferred_element_type=jnp.fl...  34.1 us
    reshape x1, local copies, waits for them, and re-layouts, shards(): x_blocks = x_input.reshape(count, GROUP, heads, head_size)  24.4 us
    dot_general x1, matrix products, shards(): jnp.einsum('ktn,khpn->kthp', c_blocks, full_state, preferred_element_type...  16.3 us
    all_gather x2, blocking collectives, prefix_by_axis(): pieces = jax.tree.map(lambda part: lax.all_gather(part, axis), running)  15.5 us
    convert_element_type x1, local copies, waits for them, and re-layouts, shards(): y_output = mixed.astype(jnp.bfloat16).reshape(rows, width)  15.4 us
    dot_general x8, matrix products, local_block(): jnp.einsum('shp,sn->hpn', scaled, b_group, preferred_element_type=jnp.flo...  14.2 us
  transfers between devices with their start and end apart: 5, of which 4 were waited for; matrix products, arithmetic and copies ran while one was open for 5% of the time, Pallas kernels for 0%

commit v1 on v0

v1 whole, which is shorter than its diff:
```python
import functools

import jax
import jax.numpy as jnp
from jax import lax
from jax.experimental import pallas as pl
from jax.experimental.pallas import tpu as pltpu
from jax.sharding import Mesh
from jax.sharding import PartitionSpec as P

SEC_DEV = ("sec", "dev_0", "dev_1", "dev_2")
CHUNK = 64
BLOCK = 256
LANES = 128
LOG2E = 1.4426950408889634
F32 = jnp.float32
BF16 = jnp.bfloat16


def iota(shape, dim):
    return lax.broadcasted_iota(jnp.int32, shape, dim)


def mm(a, b):
    return jnp.dot(a, b, preferred_element_type=F32)


def mm_nt(a, b):
    return lax.dot_general(a, b, (((1,), (1,)), ((), ())), preferred_element_type=F32)


def split(value, pieces):
    parts = []
    for _ in range(pieces - 1):
        part = value.astype(BF16)
        parts.append(part)
        value = value - part.astype(F32)
    parts.append(value.astype(BF16))
    return parts


def trace_of(starts, position):
    total = jnp.zeros_like(position)
    for start in starts:
        total = total + jnp.where(position >= start, 1, 0)
    return total


def expander(heads, head_size, copies):
    shape = (heads * copies, heads * head_size)
    same = (iota(shape, 0) % heads) == (iota(shape, 1) // head_size)
    return jnp.where(same, 1.0, 0.0).astype(BF16)


def local_kernel(
    lengths_ref, base_ref, x_ref, decay_ref, b_ref, c_ref, skip_ref,
    y_ref, reach_ref, message_ref,
    expand_ref, cum_ref, state_ref, total_ref, skip_row_ref,
):
    step = pl.program_id(0)
    heads = decay_ref.shape[1]
    width = x_ref.shape[1]
    head_size = width // heads
    n = b_ref.shape[1]
    base = base_ref[0]
    starts = []
    first = jnp.int32(0)
    for k in range(lengths_ref.shape[0]):
        starts.append(first)
        first = first + lengths_ref[k]

    @pl.when(step == 0)
    def _():
        expand_ref[...] = expander(heads, head_size, 3)
        state_ref[...] = jnp.zeros_like(state_ref)
        total_ref[...] = jnp.zeros_like(total_ref)
        gain = jnp.concatenate(split(jnp.broadcast_to(skip_ref[...], (8, heads)), 3), axis=1)
        skip_row_ref[...] = mm(gain, expand_ref[...])

    at_block = base + step * BLOCK
    logs = split(decay_ref[...] * LOG2E, 3)
    shape = (BLOCK, BLOCK)
    lower = iota(shape, 0) >= iota(shape, 1)
    same_chunk = (iota(shape, 0) // CHUNK) == (iota(shape, 1) // CHUNK)
    ones_all = jnp.where(lower, 1.0, 0.0).astype(BF16)
    ones_chunk = jnp.where(lower & same_chunk, 1.0, 0.0).astype(BF16)
    cum = mm(ones_chunk, logs[0]) + mm(ones_chunk, logs[1]) + mm(ones_chunk, logs[2])
    far = mm(ones_all, logs[0]) + mm(ones_all, logs[1]) + mm(ones_all, logs[2])
    far = far + total_ref[0:1, :]
    total_ref[...] = jnp.broadcast_to(far[BLOCK - 1 :, :], total_ref.shape)
    before = trace_of(starts, base - 1)
    block_pos = at_block + iota((BLOCK, heads), 0)
    reach = jnp.where(trace_of(starts, block_pos) == before, jnp.exp2(far), 0.0)
    reach_ref[...] = jnp.concatenate(split(reach, 2), axis=1)
    cum_ref[...] = mm(jnp.concatenate(split(cum, 3), axis=1), expand_ref[...])

    small = (CHUNK, LANES)
    row_id = iota(small, 0)
    col_id = iota(small, 1) % CHUNK
    causal = row_id >= col_id
    diagonal = row_id == col_id
    left = jnp.where(iota(small, 1) < CHUNK, 1.0, 0.0).astype(BF16)
    right = jnp.where(iota(small, 1) >= CHUNK, 1.0, 0.0).astype(BF16)

    def chunk(k, carry):
        row = pl.multiple_of(k * CHUNK, CHUNK)
        rows = pl.ds(row, CHUNK)
        pos = at_block + row
        tr_prev = trace_of(starts, pos - 1)
        tr_end = trace_of(starts, pos + CHUNK - 1)
        keep = causal & (trace_of(starts, pos + row_id) == trace_of(starts, pos + col_id))
        token = trace_of(starts, pos + iota((CHUNK, n), 0))
        c_chunk = c_ref[rows, :]
        b_chunk = b_ref[rows, :]
        gram = mm_nt(c_chunk, jnp.concatenate([b_chunk, b_chunk], axis=0))
        gram = jnp.where(keep, gram, 0.0)
        c_mask = jnp.where(token == tr_prev, c_chunk.astype(F32), 0.0).astype(BF16)
        b_mask = jnp.where(token == tr_end, b_chunk.astype(F32), 0.0).T.astype(BF16)
        goes_on = jnp.where(tr_end == tr_prev, 1.0, 0.0)
        for pair in range(width // LANES):
            lanes = slice(pair * LANES, (pair + 1) * LANES)
            ce = cum_ref[rows, lanes]
            end = ce[CHUNK - 1 :, :]
            across = jnp.sum(jnp.where(diagonal, ce, 0.0), axis=0, keepdims=True)
            from_start = jnp.exp2(ce)
            to_end = jnp.exp2(end - ce)
            x_pair = x_ref[rows, lanes]
            x_wide = x_pair.astype(F32)
            weight = (gram * jnp.exp2(jnp.minimum(ce - across, 0.0))).astype(BF16)
            x_diag = jnp.concatenate([x_pair * left, x_pair * right], axis=0)
            intra = mm(weight, x_diag)
            held = state_ref[:, lanes]
            inter = mm(c_mask, held.astype(BF16))
            y = intra + from_start * inter + skip_row_ref[0:1, lanes] * x_wide
            y_ref[rows, lanes] = y.astype(BF16)
            scaled = (x_wide * to_end).astype(BF16)
            factor = from_start[CHUNK - 1 :, :] * goes_on
            state_ref[:, lanes] = held * factor + mm(b_mask, scaled)
        return carry

    lax.fori_loop(0, BLOCK // CHUNK, chunk, 0)

    @pl.when(step == pl.num_programs(0) - 1)
    def _():
        last = reach[BLOCK - 8 :, :]
        whole = mm(jnp.concatenate(split(last, 3), axis=1), expand_ref[...])
        pairs = width // LANES
        for i in range(n // 8):
            for j in range(pairs):
                lanes = slice(j * LANES, (j + 1) * LANES)
                tile = state_ref[8 * i : 8 * i + 8, lanes]
                for k in range(8):
                    message_ref[i * pairs + j, :, k * LANES : (k + 1) * LANES] = tile[k : k + 1, :]
                message_ref[i * pairs + j, :, 8 * LANES :] = whole[7:8, lanes]


def prefix_kernel(got_ref, out_ref):
    def one(d, held):
        got = got_ref[d]
        factor = got[:, 8 * LANES :]
        following = []
        for k in range(8):
            lanes = slice(k * LANES, (k + 1) * LANES)
            out_ref[d, :, lanes] = held[k]
            following.append(held[k] * factor + got[:, lanes])
        return tuple(following)

    zero = jnp.zeros((1, LANES), F32)
    lax.fori_loop(0, got_ref.shape[0], one, (zero,) * 8, unroll=4)


def final_kernel(
    base_ref, y_in_ref, c_ref, reach_ref, back_ref, weight_ref, start_ref, length_ref, slot_ref,
    y_ref, spread_ref,
    expand_ref, gather_ref, state_ref, score_ref, weight_row_ref,
):
    step = pl.program_id(0)
    heads = reach_ref.shape[1] // 2
    width = y_ref.shape[1]
    n = c_ref.shape[1]
    pairs = width // LANES
    tokens = BLOCK * pl.num_programs(0)

    @pl.when(step == 0)
    def _():
        expand_ref[...] = expander(heads, width // heads, 2)
        weight_row_ref[...] = jnp.broadcast_to(
            weight_ref[...].astype(F32), weight_row_ref.shape
        )
        for i in range(n // 8):
            for j in range(pairs):
                piece = back_ref[i * pairs + j]
                for k in range(8):
                    gather_ref[8 * i + k : 8 * i + k + 1, j * LANES : (j + 1) * LANES] = piece[
                        :, k * LANES : (k + 1) * LANES
                    ]
        state_ref[...] = gather_ref[...].astype(BF16)

    c_block = c_ref[...]
    reach = reach_ref[...]
    total = jnp.zeros((BLOCK, LANES), F32)
    wide = 2 * LANES
    for part in range(width // wide):
        lanes = slice(part * wide, (part + 1) * wide)
        inter = mm(c_block, state_ref[:, lanes])
        gain = mm(reach, expand_ref[:, lanes])
        y = y_in_ref[:, lanes].astype(F32) + gain * inter
        y_ref[:, lanes] = y.astype(BF16)
        scored = y * weight_row_ref[0:1, lanes]
        total = total + scored[:, :LANES] + scored[:, LANES:]
    for k in range(BLOCK // LANES):
        turned = total[k * LANES : (k + 1) * LANES, :].T
        score_ref[pl.ds(step * (BLOCK // LANES) + k, 1), :] = jnp.sum(turned, axis=0, keepdims=True)

    @pl.when(step == pl.num_programs(0) - 1)
    def _():
        base = base_ref[0]
        steps = slot_ref.shape[1]
        slot_rows = steps // LANES
        slot = slot_ref[...]
        at = start_ref[...]
        span = length_ref[...]
        in_row = jnp.where(
            iota((slot_rows, steps), 0) == (slot >> 7), 1.0, 0.0
        )
        in_lane = jnp.where(iota((LANES, steps), 0) == (slot & 127), 1.0, 0.0).astype(BF16)
        found = []
        for value in (at >> 16, (at >> 8) & 255, at & 255, span >> 8, span & 255):
            found.append(mm_nt((in_row * value.astype(F32)).astype(BF16), in_lane))
        start = (found[0] * 65536.0 + found[1] * 256.0 + found[2]).astype(jnp.int32)
        length_f = found[3] * 256.0 + found[4]
        length = length_f.astype(jnp.int32)
        from_tok = jnp.clip(start - base, 0, tokens)
        to_tok = jnp.clip(start + length - base, 0, tokens)

        held = score_ref.shape[0]
        grown = held + 8
        score = score_ref[...]
        strict = jnp.where(iota((LANES, LANES), 0) < iota((LANES, LANES), 1), 1.0, 0.0)
        strict = strict.astype(BF16)
        ahead = jnp.where(iota((grown, held), 1) < iota((grown, held), 0), 1.0, 0.0).astype(BF16)
        inside = jnp.zeros((held, LANES), F32)
        offset = jnp.zeros((grown, LANES), F32)
        for piece in split(score, 3):
            inside = inside + mm(piece, strict)
            offset = offset + mm(ahead, piece)
        running = jnp.sum(offset, axis=1, keepdims=True) + jnp.concatenate(
            [inside, jnp.zeros((8, LANES), F32)], axis=0
        )
        table = split(running, 3)

        def look_up(index):
            pick = jnp.where(iota((LANES, LANES), 0) == (index & 127), 1.0, 0.0).astype(BF16)
            rows = mm(table[0], pick) + mm(table[1], pick) + mm(table[2], pick)
            mine = iota((grown, LANES), 0) == (index >> 7)
            return jnp.sum(jnp.where(mine, rows, 0.0), axis=0, keepdims=True)

        for r in range(slot_rows):
            value = look_up(to_tok[r : r + 1, :]) - look_up(from_tok[r : r + 1, :])
            spread_ref[r : r + 1, :] = value / length_f[r : r + 1, :]


def shards(
    x_input,
    log_decay,
    b_input,
    c_input,
    skip_gain,
    score_weight,
    trace_lengths,
    step_lengths,
    step_slot,
):
    rows, width = x_input.shape
    heads = log_decay.shape[1]
    n = b_input.shape[1]
    devices = lax.axis_size(SEC_DEV)
    index = lax.axis_index(SEC_DEV)
    base = (index * rows).astype(jnp.int32).reshape(1)
    blocks = rows // BLOCK
    tiles = (n // 8) * (width // LANES)
    smem = pl.BlockSpec(memory_space=pltpu.SMEM)

    def by_block(columns):
        return pl.BlockSpec((BLOCK, columns), lambda i: (i, 0))

    def whole(*shape):
        return pl.BlockSpec(shape, lambda i: (0,) * len(shape))

    params = pltpu.CompilerParams(
        dimension_semantics=("arbitrary",), vmem_limit_bytes=40 * 1024 * 1024
    )
    y_local, reach, message = pl.pallas_call(
        local_kernel,
        grid=(blocks,),
        in_specs=[
            smem, smem, by_block(width), by_block(heads), by_block(n), by_block(n), whole(1, heads),
        ],
        out_specs=[by_block(width), by_block(2 * heads), whole(tiles, 1, 9 * LANES)],
        out_shape=[
            jax.ShapeDtypeStruct((rows, width), BF16),
            jax.ShapeDtypeStruct((rows, 2 * heads), BF16),
            jax.ShapeDtypeStruct((tiles, 1, 9 * LANES), F32),
        ],
        scratch_shapes=[
            pltpu.VMEM((3 * heads, width), BF16),
            pltpu.VMEM((BLOCK, width), F32),
            pltpu.VMEM((n, width), F32),
            pltpu.VMEM((8, heads), F32),
            pltpu.VMEM((8, width), F32),
        ],
        compiler_params=params,
        name="local",
    )(trace_lengths, base, x_input, log_decay, b_input, c_input, skip_gain.reshape(1, heads))
    arrived = lax.all_to_all(message, SEC_DEV, split_axis=0, concat_axis=0, tiled=True)
    incoming = pl.pallas_call(
        prefix_kernel,
        out_shape=jax.ShapeDtypeStruct((devices, 1, 8 * LANES), F32),
        in_specs=[pl.BlockSpec(memory_space=pltpu.VMEM)],
        out_specs=pl.BlockSpec(memory_space=pltpu.VMEM),
        compiler_params=pltpu.CompilerParams(vmem_limit_bytes=8 * 1024 * 1024),
        name="prefix",
    )(arrived)
    back = lax.all_to_all(incoming, SEC_DEV, split_axis=0, concat_axis=0, tiled=True)
    steps = step_slot.shape[0]
    step_starts = (jnp.cumsum(step_lengths) - step_lengths).astype(jnp.int32)
    y_output, spread = pl.pallas_call(
        final_kernel,
        grid=(blocks,),
        in_specs=[
            smem, by_block(width), by_block(n), by_block(2 * heads),
            whole(tiles, 1, 8 * LANES), whole(1, width), whole(1, steps), whole(1, steps),
            whole(1, steps),
        ],
        out_specs=[by_block(width), whole(steps // LANES, LANES)],
        out_shape=[
            jax.ShapeDtypeStruct((rows, width), BF16),
            jax.ShapeDtypeStruct((steps // LANES, LANES), F32),
        ],
        scratch_shapes=[
            pltpu.VMEM((2 * heads, width), BF16),
            pltpu.VMEM((n, width), F32),
            pltpu.VMEM((n, width), BF16),
            pltpu.VMEM((rows // LANES, LANES), F32),
            pltpu.VMEM((8, width), F32),
        ],
        compiler_params=params,
        name="final",
    )(
        base, y_local, c_input, reach, back, score_weight.reshape(1, width),
        step_starts.reshape(1, steps), step_lengths.reshape(1, steps), step_slot.reshape(1, steps),
    )
    owned = steps // devices
    received = lax.all_to_all(
        spread.reshape(devices, 1, owned), SEC_DEV, split_axis=0, concat_axis=0, tiled=True
    )
    return (y_output, jnp.sum(received, axis=(0, 1)))


def solution(mesh):
    torus = Mesh(
        mesh.devices.reshape(mesh.shape["sec"], 4, 4, 2), ("sec", "dev_0", "dev_1", "dev_2")
    )
    in_specs = (P(SEC_DEV, None),) * 4 + (P(),) * 5
    out_specs = (P(SEC_DEV, None), P(SEC_DEV))
    return jax.shard_map(
        shards, mesh=torus, in_specs=in_specs, out_specs=out_specs, check_vma=False
    )
```

time: 406 us -> 111 us (0.27)
  waiting for transfers between devices: 129 us -> 13 us
  local copies, waits for them, and re-layouts: 99.7 us -> 12.1 us
  matrix products: 79.1 us -> 0 us
  other arithmetic: 43.7 us -> 1.06 us
  Pallas kernels: 0 us -> 39.4 us
  between operations: 15.3 us -> 0.77 us
  blocking collectives: 27.6 us -> 39.4 us
  starting transfers between devices: 8.78 us -> 4.54 us
    all_gather x4 -> x0, waiting for transfers between devices: 129 us -> none  [prefix_by_axis(): pieces = jax.tree.map(lambda part: lax.all_gather(part, axis), running)]
    dot_general x38 -> x0, matrix products: 79.1 us -> none  [the longest x8 34.1 us: local_block(): jnp.einsum('hts,shp->thp', weight, x_heads, preferred_element_type=jnp.fl...]
    all_to_all x0 -> x2, blocking collectives: none -> 39.4 us  [the longest x1 25.5 us: shards(): lax.all_to_all(message, SEC_DEV, split_axis=0, concat_axis=0, tiled=True)]
    pallas_call x0 -> x3, Pallas kernels: none -> 39.4 us  [the longest x1 28.1 us: shards(): pl.pallas_call(local_kernel, grid=(blocks,), in_specs=[smem, smem, by_blo...]
    unnamed x33 -> x17, local copies, waits for them, and re-layouts: 45.2 us -> 11.8 us
    reshape x3 -> x2, local copies, waits for them, and re-layouts: 25.4 us -> 0.08 us  [the longest x1 0.07 us: shards(): spread.reshape(devices, 1, owned)]
    all_gather x2 -> x0, blocking collectives: 15.5 us -> none  [prefix_by_axis(): pieces = jax.tree.map(lambda part: lax.all_gather(part, axis), running)]
    convert_element_type x1 -> x0, local copies, waits for them, and re-layouts: 15.4 us -> none  [shards(): y_output = mixed.astype(jnp.bfloat16).reshape(rows, width)]
  transfers between devices with their start and end apart: 5 -> 1, of which waited for: 4 -> 1; matrix products, arithmetic and copies ran while one was open for 5% -> 1% of each run, Pallas kernels for 0% -> 0%
where the time goes in v1:
time: 111 us; the launch traced here: 110 us
  Pallas kernels  39.4 us (35%)
  blocking collectives  39.4 us (35%)
  waiting for transfers between devices  13 us (12%)
  local copies, waits for them, and re-layouts  12.1 us (11%)
  starting transfers between devices  4.54 us (4%)
    pallas_call x1, Pallas kernels, shards(): pl.pallas_call(local_kernel, grid=(blocks,), in_specs=[smem, smem, by_blo...  28.1 us
    all_to_all x1, blocking collectives, shards(): lax.all_to_all(message, SEC_DEV, split_axis=0, concat_axis=0, tiled=True)  25.5 us
    all_to_all x1, blocking collectives, shards(): lax.all_to_all(spread.reshape(devices, 1, owned), SEC_DEV, split_axis=0,...  14 us
    all_to_all x1, waiting for transfers between devices, shards(): lax.all_to_all(incoming, SEC_DEV, split_axis=0, concat_axis=0, tiled=True)  13 us
    unnamed x17, local copies, waits for them, and re-layouts  11.8 us
    pallas_call x1, Pallas kernels, shards(): pl.pallas_call(final_kernel, grid=(blocks,), in_specs=[smem, by_block(wid...  9.98 us
    all_to_all x1, starting transfers between devices, shards(): lax.all_to_all(incoming, SEC_DEV, split_axis=0, concat_axis=0, tiled=True)  4.54 us
  transfers between devices with their start and end apart: 1, of which 1 were waited for; matrix products, arithmetic and copies ran while one was open for 1% of the time, Pallas kernels for 0%

profile of v1, /device:TPU:1, one launch (start us, length us, event | category | flops | bytes accessed | tf_op | source)
XLA Modules:
  0.0 110.3 jit_solution(1781173832225321696)
XLA Ops:
  0.6 0.0 copy-start.2
  0.6 0.0 copy-start.6
  0.7 0.0 copy-start.3
  0.7 1.2 %copy.21.c_ref = bf16[2048,64]{1,0:T(8,128)(2,1)S(1)} copy(bf16[2048,64]{0,1:T(8,128)(2,1)} %param.12) | data formatting | bytes 524288 | tf_op args[3]
  1.9 1.2 %copy.20.b_ref = bf16[2048,64]{1,0:T(8,128)(2,1)S(1)} copy(bf16[2048,64]{0,1:T(8,128)(2,1)} %param.11) | data formatting | bytes 524288 | tf_op args[2]
  3.1 1.3 %copy.19.decay_ref = f32[2048,32]{1,0:T(8,128)S(1)} copy(f32[2048,32]{0,1:T(8,128)} %param.10) | data formatting | bytes 524288 | tf_op args[1]
  4.4 0.0 copy-start.4
  4.5 0.6 copy-done.4
  5.1 0.0 copy-start.5
  5.1 0.7 copy-done.5
  5.8 28.1 %local.1 = (bf16[2048,2048]{1,0:T(8,128)(2,1)S(1)}, bf16[2048,64]{1,0:T(8,128)(2,1)S(1)}, f32[128,1,1152]{2,1,0:T(1,128)S(1)}) custom-call(s32[4]{0:T(128)S(1)} %copy-done.4, s32[1]{0:T(128)} %bitcast.base_ref, bf16[2048,2048]{1,0:T(8,128)(2,1)} %x_ref.1, f32[2048,32]{1,0:T(8,128)S(1)} %copy.19.decay_ref, bf16[2048,64]{1,0:T(8,128)(2,1)S(1)} %copy.20.b_ref, ...), custom_call_target="tpu_custom_call" | custom-call | tf_op jit(solution)/shard_map/local/pallas_call | solution.py:293
  33.9 0.0 copy-start
  33.9 3.4 %copy-done = bf16[2048,2048]{1,0:T(8,128)(2,1)} copy-done((bf16[2048,2048]{1,0:T(8,128)(2,1)}, bf16[2048,2048]{1,0:T(8,128)(2,1)S(1)}, u32[]{:S(2)}) %copy-start) | copy-done | bytes 8388632
  37.3 25.5 %all_to_all.15.got_ref = f32[128,1,1152]{2,1,0:T(1,128)S(1)} all-to-all(f32[128,1,1152]{2,1,0:T(1,128)S(1)} %get-tuple-element.9), channel_id=1, replica_groups=mesh['sec'=4,'dev_0'=4,'dev_1'=4,'dev_2'=2] {'sec','dev_0','dev_1','dev_2'}, dimensions={0} | all-to-all | bytes 1179648 | tf_op jit(solution)/shard_map/all_to_all | solution.py:315
  62.8 1.3 %prefix.1 = f32[128,1,1024]{2,1,0:T(1,128)} custom-call(f32[128,1,1152]{2,1,0:T(1,128)S(1)} %all_to_all.15.got_ref), custom_call_target="tpu_custom_call" | custom-call | tf_op jit(solution)/shard_map/prefix/pallas_call | solution.py:316
  64.1 4.5 %all-to-all-start.1 = ((f32[128,1,1024]{2,1,0:T(1,128)}), f32[128,1,1024]{2,1,0:T(1,128)S(1)}, u32[]{:S(2)}, u32[]{:S(2)}) async-start(f32[128,1,1024]{2,1,0:T(1,128)} %prefix.1), calls=%async_computation.1 | async-start | bytes 1048576 | tf_op jit(solution)/shard_map/all_to_all | solution.py:324
  68.6 0.0 copy-done.2
  68.6 0.3 reduce-window.9
  68.9 0.1 slice.9
  69.0 0.0 copy-done.6
  69.1 0.1 slice_reduce_fusion
  69.2 0.1 bitcast_subtract_fusion
  69.2 13.0 %all-to-all-done.1.back_ref = f32[128,1,1024]{2,1,0:T(1,128)S(1)} async-done(((f32[128,1,1024]{2,1,0:T(1,128)}), f32[128,1,1024]{2,1,0:T(1,128)S(1)}, u32[]{:S(2)}, u32[]{:S(2)}) %all-to-all-start.1) | async-done | bytes 524320 | tf_op jit(solution)/shard_map/all_to_all | solution.py:324
  82.2 0.0 copy-done.3
  82.2 0.0 copy-start.1
  82.2 3.4 %copy-done.1 = bf16[2048,2048]{1,0:T(8,128)(2,1)S(1)} copy-done((bf16[2048,2048]{1,0:T(8,128)(2,1)S(1)}, bf16[2048,2048]{1,0:T(8,128)(2,1)}, u32[]{:S(2)}) %copy-start.1) | copy-done | bytes 8388632
  85.6 10.0 %final.1 = (bf16[2048,2048]{1,0:T(8,128)(2,1)}, f32[16,128]{1,0:T(8,128)S(1)}) custom-call(s32[1]{0:T(128)} %bitcast.base_ref, bf16[2048,2048]{1,0:T(8,128)(2,1)S(1)} %copy-done.1, bf16[2048,64]{1,0:T(8,128)(2,1)S(1)} %copy.21.c_ref, bf16[2048,64]{1,0:T(8,128)(2,1)S(1)} %get-tuple-element.8.reach_ref, f32[128,1,1024]{2,1,0:T(1,128)S(1)} %all-to-all-done.1.back_ref, ...), custom_call_target="tpu_custom_call" | custom-call | tf_op jit(solution)/shard_map/final/pallas_call | solution.py:327
  95.6 0.1 reshape.47
  95.7 14.0 %all_to_all.16 = f32[128,1,16]{2,1,0:T(1,128)S(1)} all-to-all(f32[128,1,16]{2,1,0:T(1,128)S(1)} %bitcast.14), channel_id=1, replica_groups=mesh['sec'=4,'dev_0'=4,'dev_1'=4,'dev_2'=2] {'sec','dev_0','dev_1','dev_2'}, dimensions={0} | all-to-all | bytes 16384 | tf_op jit(solution)/shard_map/all_to_all | solution.py:354
  109.7 0.7 reduce_sum.9
  (2 shorter events, 0.0 us)
Async XLA Ops:
  0.6 68.0 %copy-start.2 = (s32[2048]{0:T(1024)S(1)}, s32[2048]{0:T(1024)}, u32[]{:S(2)}) copy-start(s32[2048]{0:T(1024)} %param.16) | copy-start | bytes 24580
  0.6 68.4 %copy-start.6 = (bf16[2048]{0:T(1024)(128)(2,1)S(1)}, bf16[2048]{0:T(1024)(128)(2,1)}, u32[]{:S(2)}) copy-start(bf16[2048]{0:T(1024)(128)(2,1)} %param.14) | copy-start | bytes 12292
  0.7 81.6 %copy-start.3 = (s32[2048]{0:T(1024)S(1)}, s32[2048]{0:T(1024)}, u32[]{:S(2)}) copy-start(s32[2048]{0:T(1024)} %param.17) | copy-start | bytes 24580
  4.4 0.7 copy-start.4
  5.1 0.7 copy-start.5
  33.9 3.4 %copy-start = (bf16[2048,2048]{1,0:T(8,128)(2,1)}, bf16[2048,2048]{1,0:T(8,128)(2,1)S(1)}, u32[]{:S(2)}) copy-start(bf16[2048,2048]{1,0:T(8,128)(2,1)S(1)} %get-tuple-element.7.y_in_ref) | copy-start | bytes 25165828
  64.1 18.2 %all-to-all-start.1 = ((f32[128,1,1024]{2,1,0:T(1,128)}), f32[128,1,1024]{2,1,0:T(1,128)S(1)}, u32[]{:S(2)}, u32[]{:S(2)}) async-start(f32[128,1,1024]{2,1,0:T(1,128)} %prefix.1), calls=%async_computation.1 | async-start | bytes 1048576 | tf_op jit(solution)/shard_map/all_to_all | solution.py:324
  82.2 3.4 %copy-start.1 = (bf16[2048,2048]{1,0:T(8,128)(2,1)S(1)}, bf16[2048,2048]{1,0:T(8,128)(2,1)}, u32[]{:S(2)}) copy-start(bf16[2048,2048]{1,0:T(8,128)(2,1)} %copy-done) | copy-start | bytes 25165828
